TPU v7x, 512 devices: a whole 4x4x16 slice. The times are simulated.
512 devices in a mesh: row: 32 (over z, core), col: 16 (over x, y).
Axes of the slice: x: 4, y: 4, z: 16, core: 2. Of those that a mesh axis runs over, the one named last changes fastest.
Arguments:
- front_entries: float32 [16384, 16384], P('row', 'col'), may hold values from 0 to 3, as said below
- tile_group: int32 [32], replicated, may hold values from 0 to 3
- child_factor: bfloat16 [16384, 256], P('row', 'col'), may hold values from -0.375 to 0.375
- row_map: int32 [128], replicated, may hold values from 0 to 127, as said below
Outputs:
- factor_panels: bfloat16 [16384, 512], P('row', 'col')
- schur_block: float32 [16384, 16384], P('row', 'col')
Inputs may be any that keep to these rules, and one draw needn't show every extreme that they name: `front_entries`: Symmetric; assembled is positive definite. `row_map`: A permutation of the parent tiles. The tile in row block r (blocks of 512 rows) goes to a parent tile in row block r or in the row block whose index differs from r in the highest bit.
All inputs are finite; a program needn't handle non-finite values.
Results may differ from a plain program's by a relative error of at most 0.0026.
Values may be sent and summed in bfloat16 or wider, within the bound.
A program may use at most 64 MiB of HBM per device.

v0:
```python
import jax
import jax.numpy as jnp
from jax import lax
from jax.sharding import PartitionSpec as P

PW = 256
NP = 2
TS = 128
MT = 512


def swapped(value, axis, stride):
    mask = 2**stride
    pairs = [(source, source ^ mask) for source in range(lax.axis_size(axis))]
    return lax.ppermute(value, axis, pairs)


def broadcast(value, axis, source):
    kept = jnp.where(lax.axis_index(axis) == source, value, 0).astype(value.dtype)
    return lax.psum(kept, axis)


def panel_columns(matrix, offset, width_cols, fan_ratio, block_rows):
    return jnp.concatenate(
        [
            matrix[:, q * block_rows + offset : q * block_rows + offset + width_cols]
            for q in range(fan_ratio)
        ],
        axis=1,
    )


def outer_rows(left, right):
    return jnp.einsum("ik,jk->ij", left, right, preferred_element_type=jnp.float32)


def subtract_block(matrix, lead_rows, owner, low, col_from, col_to, base_col):
    region = matrix[low:, base_col + col_from : base_col + col_to]
    return matrix.at[low:, base_col + col_from : base_col + col_to].set(
        region - outer_rows(lead_rows, owner[col_from:col_to])
    )


def right_solve(lower_factor, strip):
    return lax.linalg.triangular_solve(
        lower_factor, strip, left_side=False, lower=True, transpose_a=True
    )


def local(front_entries, tile_group, child_factor, row_map):
    row_count = lax.axis_size("row")
    col_count = lax.axis_size("col")
    fan_ratio = row_count // col_count
    local_rows = front_entries.shape[0]
    local_cols = front_entries.shape[1]
    my_row = lax.axis_index("row")
    my_col = lax.axis_index("col")
    row_tiles = local_rows // MT
    col_tiles = local_cols // MT
    group_rows = lax.dynamic_slice_in_dim(tile_group, my_row * row_tiles, row_tiles)
    group_cols = lax.dynamic_slice_in_dim(tile_group, my_col * col_tiles, col_tiles)
    same_group = (group_rows[:, None] == group_cols[None, :]).astype(jnp.float32)
    masked = (
        front_entries.reshape(row_tiles, MT, col_tiles, MT) * same_group[:, None, :, None]
    ).reshape(local_rows, local_cols)
    child_full = lax.all_gather(child_factor, "col", axis=1, tiled=True)
    child_width = child_full.shape[1]
    partner_full = swapped(child_full, "row", row_count.bit_length() - 2)
    tile_count = local_rows // TS
    partner_row = jnp.bitwise_xor(my_row, row_count // 2)
    own_map = lax.dynamic_slice_in_dim(row_map, my_row * tile_count, tile_count)
    partner_map = lax.dynamic_slice_in_dim(row_map, partner_row * tile_count, tile_count)
    slot_ids = my_row * tile_count + jnp.arange(tile_count, dtype=jnp.int32)

    def place_tiles(tile_map, source):
        chooser = (tile_map[None, :] == slot_ids[:, None]).astype(jnp.bfloat16)
        placed = jnp.dot(
            chooser,
            source.reshape(tile_count, TS * child_width),
            preferred_element_type=jnp.float32,
        )
        return placed.astype(jnp.bfloat16).reshape(local_rows, child_width)

    own_parent = place_tiles(own_map, child_full)
    partner_parent = place_tiles(partner_map, partner_full)
    lower_half = my_row < row_count // 2
    child_wide = jnp.where(
        lower_half,
        jnp.concatenate([own_parent, partner_parent], axis=1),
        jnp.concatenate([partner_parent, own_parent], axis=1),
    )
    child_owners = [broadcast(child_wide, "row", fan_ratio * my_col + q) for q in range(fan_ratio)]
    matrix = jnp.concatenate(
        [
            masked[:, q * local_rows : (q + 1) * local_rows]
            + outer_rows(child_wide, child_owners[q])
            for q in range(fan_ratio)
        ],
        axis=1,
    )
    row_share = PW // row_count
    col_share = PW // col_count
    local_ids = jnp.arange(local_rows)
    coming = None
    outputs = []
    for k in range(NP):
        offset = k * row_share
        panel_strip = panel_columns(matrix, offset, row_share, fan_ratio, local_rows)
        corner = panel_strip[offset : offset + row_share]
        gathered = lax.all_gather(corner, ("row", "col"), axis=0, tiled=True)
        diagonal = (
            gathered.reshape(row_count, col_count, row_share, col_share)
            .transpose(0, 2, 1, 3)
            .reshape(PW, PW)
        )
        lower_factor = jnp.linalg.cholesky(diagonal)
        whole_strip = lax.all_gather(panel_strip, "col", axis=1, tiled=True)
        rounded = right_solve(lower_factor, whole_strip).astype(jnp.bfloat16)
        own_lower = lax.dynamic_slice_in_dim(lower_factor, my_row * row_share, row_share).astype(
            jnp.bfloat16
        )
        rounded = jnp.where((local_ids < offset)[:, None], jnp.zeros_like(rounded), rounded)
        rounded = rounded.at[offset : offset + row_share].set(own_lower)
        outputs.append(lax.dynamic_slice_in_dim(rounded, my_col * col_share, col_share, 1))
        owners = [broadcast(rounded, "row", fan_ratio * my_col + q) for q in range(fan_ratio)]
        low = offset + row_share
        lead_rows = rounded[low:]
        for q in range(fan_ratio):
            matrix = subtract_block(
                matrix, lead_rows, owners[q], low, low, local_rows, q * local_rows
            )
    pivot_done = NP * row_share
    row_keep = local_ids >= pivot_done
    col_keep = jnp.arange(local_cols) % local_rows >= pivot_done
    schur_block = jnp.where(row_keep[:, None] & col_keep[None, :], matrix, jnp.zeros_like(matrix))
    factor_panels = jnp.concatenate(outputs, axis=1)
    return (factor_panels, schur_block)


def solution(mesh):
    placed = (P("row", "col"), P(), P("row", "col"), P())
    return jax.shard_map(
        local,
        mesh=mesh,
        in_specs=placed,
        out_specs=(P("row", "col"), P("row", "col")),
        check_vma=False,
    )
```

profile of v0, /device:TPU:1, one launch (start us, length us, event | category | flops | bytes accessed | tf_op | source)
XLA Modules:
  0.0 1302.7 jit_solution(17513636110733798873)
XLA Ops:
  7.2 19.7 %all_gather.15 = bf16[512,256]{0,1:T(8,128)(2,1)S(1)} all-gather(bf16[512,16]{0,1:T(8,128)(2,1)} %param.21), channel_id=1, replica_groups=mesh['row'=32,'col'=16] {'col'}, dimensions={1}, use_global_device_ids=true | all-gather | bytes 278528 | tf_op jit(solution)/shard_map/all_gather | solution.py:66
  26.9 15.4 %collective-permute-start = (bf16[512,256]{0,1:T(8,128)(2,1)S(1)}, bf16[512,256]{0,1:T(8,128)(2,1)S(1)}, u32[]{:S(2)}, u32[]{:S(2)}) collective-permute-start(bf16[512,256]{0,1:T(8,128)(2,1)S(1)} %all_gather.15), channel_id=1, source_target_pairs={{0,256},{16,272},{32,288},{48,304},{64,320},{80,336},{96,352},{112... | collective-permute-start | bytes 786440 | tf_op jit(solution)/shard_map/ppermute | solution.py:15
  42.7 0.8 fusion.44
  44.1 0.6 dynamic_slice.24
  44.7 0.7 compare_convert_fusion
  45.5 1.9 copy.30
  48.3 1.3 broadcast_select_fusion.1
  49.6 1.5 broadcast_multiply_fusion
  51.2 226.5 %all-reduce.12.cloned.1.call-done = (bf16[512,512]{1,0:T(8,128)(2,1)}, bf16[512,512]{1,0:T(8,128)(2,1)}) async-done(((bf16[512,512]{1,0:T(8,128)(2,1)}, bf16[512,512]{1,0:T(8,128)(2,1)}), (bf16[512,512]{1,0:T(8,128)(2,1)}, bf16[512,512]{1,0:T(8,128)(2,1)})) %all-reduce.12.cloned.1.call-update) | async-done | bytes 1048592 | tf_op jit(solution)/shard_map/psum | solution.py:20
  277.7 2.1 convolution_add_fusion.1
  279.8 0.5 convolution_add_fusion
  280.3 1.0 copy-done.1
  281.4 198.2 %all_gather.16 = f32[4096,16]{1,0:T(8,128)S(1)} all-gather(f32[8,16]{1,0:T(8,128)S(1)} %copy.33), channel_id=1, replica_groups=mesh['row'=32,'col'=16] {'row','col'}, dimensions={0}, use_global_device_ids=true | all-gather | bytes 262656 | tf_op jit(solution)/shard_map/all_gather | solution.py:110
  479.9 0.9 reshape.255
  481.1 11.7 cholesky.130
  492.8 9.8 custom-call.13
  503.1 11.9 cholesky.147
  515.0 0.6 compare_reduce_fusion.2
  515.7 0.6 compare_reduce_fusion.3
  517.6 3.8 while.10
  517.7 0.6 fusion.59
  518.2 1.3 bitcast_dynamic-update-slice_fusion.4
  519.6 0.6 fusion.59
  520.2 1.3 bitcast_dynamic-update-slice_fusion.4
  521.5 19.7 %custom-call.14 = f32[2,128,128]{1,2,0:T(8,128)S(1)} custom-call(f32[2,128,128]{2,1,0:T(8,128)S(1)} %get-tuple-element.90), custom_call_target="InvertDiagBlocksLowerTriangular" | custom-call | tf_op jit(solution)/shard_map/triangular_solve/custom-call.0 | solution.py:45
  541.2 16.2 %all_gather.17 = f32[512,256]{0,1:T(8,128)S(1)} all-gather(f32[512,16]{0,1:T(8,128)S(1)} %pad_maximum_fusion.1), channel_id=1, replica_groups=mesh['row'=32,'col'=16] {'col'}, dimensions={1}, use_global_device_ids=true | all-gather | bytes 557056 | tf_op jit(solution)/shard_map/all_gather | solution.py:117
  557.4 0.4 fusion.7
  557.8 0.4 convolution_subtract_fusion.5
  558.2 0.4 fusion.22
  559.1 0.8 broadcast_select_fusion.3
  560.0 1.4 pad_maximum_fusion
  561.5 209.2 %all-reduce.10.cloned.1.call-done = (bf16[512,256]{0,1:T(8,128)(2,1)}, bf16[512,256]{0,1:T(8,128)(2,1)}) async-done(((bf16[512,256]{0,1:T(8,128)(2,1)}, bf16[512,256]{0,1:T(8,128)(2,1)}), (bf16[512,256]{0,1:T(8,128)(2,1)}, bf16[512,256]{0,1:T(8,128)(2,1)})) %all-reduce.10.cloned.1.call-update) | async-done | bytes 524304 | tf_op jit(solution)/shard_map/psum | solution.py:20
  770.6 2.6 convolution_subtract_fusion.1
  773.2 5.4 scatter.21
  778.6 1.6 convolution_subtract_fusion
  780.2 3.4 scatter.24
  783.8 197.6 %all_gather.18 = f32[4096,16]{1,0:T(8,128)S(1)} all-gather(f32[8,16]{1,0:T(8,128)S(1)} %copy.38), channel_id=1, replica_groups=mesh['row'=32,'col'=16] {'row','col'}, dimensions={0}, use_global_device_ids=true | all-gather | bytes 262656 | tf_op jit(solution)/shard_map/all_gather | solution.py:110
  981.5 1.7 copy.39
  983.2 2.6 reshape.257
  986.0 11.7 cholesky.164
  997.8 9.8 custom-call.15
  1008.1 11.7 cholesky.181
  1019.8 0.6 compare_reduce_fusion
  1020.5 0.6 compare_reduce_fusion.1
  1022.4 4.0 while.11
  1022.5 0.6 fusion.60
  1023.1 1.4 bitcast_dynamic-update-slice_fusion.5
  1024.5 0.6 fusion.60
  1025.1 1.4 bitcast_dynamic-update-slice_fusion.5
  1026.5 19.9 %custom-call.16 = f32[2,128,128]{1,2,0:T(8,128)S(1)} custom-call(f32[2,128,128]{2,1,0:T(8,128)S(1)} %get-tuple-element.91), custom_call_target="InvertDiagBlocksLowerTriangular" | custom-call | tf_op jit(solution)/shard_map/triangular_solve/custom-call.0 | solution.py:45
  1046.4 16.3 %all_gather.19 = f32[512,256]{0,1:T(8,128)S(1)} all-gather(f32[512,16]{0,1:T(8,128)S(1)} %pad_maximum_fusion.2), channel_id=1, replica_groups=mesh['row'=32,'col'=16] {'col'}, dimensions={1}, use_global_device_ids=true | all-gather | bytes 557056 | tf_op jit(solution)/shard_map/all_gather | solution.py:117
  1062.6 0.4 fusion.3
  1063.1 0.4 convolution_subtract_fusion.4
  1063.5 0.4 fusion.18
  1064.1 0.6 scatter.25
  1064.7 0.8 broadcast_select_fusion.2
  1065.6 0.6 pad_maximum_fusion.3
  1066.2 210.0 %all-reduce.8.cloned.1.call-done = (bf16[512,256]{0,1:T(8,128)(2,1)}, bf16[512,256]{0,1:T(8,128)(2,1)}) async-done(((bf16[512,256]{0,1:T(8,128)(2,1)}, bf16[512,256]{0,1:T(8,128)(2,1)}), (bf16[512,256]{0,1:T(8,128)(2,1)}, bf16[512,256]{0,1:T(8,128)(2,1)})) %all-reduce.8.cloned.1.call-update) | async-done | bytes 524304 | tf_op jit(solution)/shard_map/psum | solution.py:20
  1276.2 2.6 convolution_subtract_fusion.3
  1278.8 5.4 scatter.26
  1284.2 1.6 convolution_subtract_fusion.2
  1285.8 5.6 scatter.29
  1291.4 1.6 and_select_fusion
  1293.0 2.9 copy.45
  (78 shorter events, 4.9 us)
Async XLA Ops:
  7.2 36.9 %copy-start.5 = (s32[32]{0:T(128)S(1)}, s32[32]{0:T(128)}, u32[]{:S(2)}) copy-start(s32[32]{0:T(128)} %param.20) | copy-start | bytes 388
  7.2 270.5 %all-reduce.12.cloned.1.call-start = ((), (), s32[]{:S(2)}) async-start(), calls=%async_computation.2 | async-start | bytes 2097152 | tf_op jit(solution)/shard_map/psum | solution.py:20
  26.9 20.5 %collective-permute-start = (bf16[512,256]{0,1:T(8,128)(2,1)S(1)}, bf16[512,256]{0,1:T(8,128)(2,1)S(1)}, u32[]{:S(2)}, u32[]{:S(2)}) collective-permute-start(bf16[512,256]{0,1:T(8,128)(2,1)S(1)} %all_gather.15), channel_id=1, source_target_pairs={{0,256},{16,272},{32,288},{48,304},{64,320},{80,336},{96,352},{112... | collective-permute-start | bytes 786440 | tf_op jit(solution)/shard_map/ppermute | solution.py:15
  48.3 2.9 copy-start.2
  49.6 721.1 %all-reduce.10.cloned.1.call-start = ((), (), s32[]{:S(2)}) async-start(), calls=%async_computation.1 | async-start | bytes 1048576 | tf_op jit(solution)/shard_map/psum | solution.py:20
  51.2 228.6 %copy-start = (f32[512,1024]{0,1:T(8,128)S(1)}, f32[512,1024]{0,1:T(8,128)}, u32[]{:S(2)}) copy-start(f32[512,1024]{0,1:T(8,128)} %broadcast_multiply_fusion) | copy-start | bytes 6291460
  277.7 2.1 copy-start.3
  277.7 2.1 copy-start.6
  280.3 1.0 copy-start.1
  560.0 716.2 %all-reduce.8.cloned.1.call-start = ((), (), s32[]{:S(2)}) async-start(), calls=%async_computation | async-start | bytes 1048576 | tf_op jit(solution)/shard_map/psum | solution.py:20
  1276.2 8.0 copy-start.4
Sparse Core Ops, SparseCore 0:
  49.7 227.9 all-reduce.11
  560.1 210.4 all-reduce.9
  1065.7 210.4 all-reduce.7
where the time goes:
time: 1310 us; the launch traced here: 1300 us
  waiting for transfers between devices  646 us (49%)
  blocking collectives  448 us (34%)
  other arithmetic  119 us (9%)
  local copies, waits for them, and re-layouts  42.4 us (3%)
  between operations  17.1 us (1%)
  starting transfers between devices  15.5 us (1%)
  matrix products  15 us (1%)
    psum x3, waiting for transfers between devices, broadcast(): return lax.psum(kept, axis)  646 us
    all_gather x2, blocking collectives, local(): gathered = lax.all_gather(corner, ('row', 'col'), axis=0, tiled=True)  396 us
    another operation x14, other arithmetic, local(): lower_factor = jnp.linalg.cholesky(diagonal)  69.3 us
    another operation x5, other arithmetic, right_solve(): lax.linalg.triangular_solve(lower_factor, strip, left_side=False, lower=T...  39.7 us
    all_gather x2, blocking collectives, local(): whole_strip = lax.all_gather(panel_strip, 'col', axis=1, tiled=True)  32.5 us
  transfers between devices with their start and end apart: 4, of which 3 were waited for; matrix products, arithmetic and copies ran while one was open for 1% of the time, Pallas kernels for 0%

commit v1 on v0

--- a/solution.py
+++ b/solution.py
@@ -9,6 +9,11 @@
 MT = 512
 
 
+def meshes_change(original, lane_axis):
+    before = lax.all_gather(original, axis_name=lane_axis)
+    return jnp.sum(before, axis=0)
+
+
 def swapped(value, axis, stride):
     mask = 2**stride
     pairs = [(source, source ^ mask) for source in range(lax.axis_size(axis))]
@@ -17,7 +22,7 @@
 
 def broadcast(value, axis, source):
     kept = jnp.where(lax.axis_index(axis) == source, value, 0).astype(value.dtype)
-    return lax.psum(kept, axis)
+    return meshes_change(kept, axis)
 
 
 def panel_columns(matrix, offset, width_cols, fan_ratio, block_rows):

time: 1310 us -> 1250 us (0.954)
  waiting for transfers between devices: 646 us -> 485 us
  other arithmetic: 119 us -> 168 us
  local copies, waits for them, and re-layouts: 42.4 us -> 83.8 us
    psum x3 -> x0, waiting for transfers between devices: 646 us -> none  [broadcast(): return lax.psum(kept, axis)]
    all_gather x0 -> x6, waiting for transfers between devices: none -> 481 us  [meshes_change(): before = lax.all_gather(original, axis_name=lane_axis)]
    reduce_sum x0 -> x6, other arithmetic: none -> 48.5 us  [meshes_change(): return jnp.sum(before, axis=0)]
    unnamed x18 -> x20, local copies, waits for them, and re-layouts: 5.87 us -> 48.1 us
  transfers between devices with their start and end apart: 4 -> 7, of which waited for: 3 -> 7; matrix products, arithmetic and copies ran while one was open for 1% -> 5% of each run, Pallas kernels for 0% -> 0%
where the time goes in v1:
time: 1250 us; the launch traced here: 1240 us
  waiting for transfers between devices  485 us (39%)
  blocking collectives  457 us (37%)
  other arithmetic  168 us (13%)
  local copies, waits for them, and re-layouts  83.8 us (7%)
  between operations  17.4 us (1%)
  starting transfers between devices  15.8 us (1%)
  matrix products  14.6 us (1%)
    all_gather x6, waiting for transfers between devices, meshes_change(): before = lax.all_gather(original, axis_name=lane_axis)  481 us
    all_gather x2, blocking collectives, local(): gathered = lax.all_gather(corner, ('row', 'col'), axis=0, tiled=True)  400 us
    another operation x14, other arithmetic, local(): lower_factor = jnp.linalg.cholesky(diagonal)  69.6 us
    reduce_sum x6, other arithmetic, meshes_change(): return jnp.sum(before, axis=0)  48.5 us
    unnamed x20, local copies, waits for them, and re-layouts  48.1 us
    another operation x5, other arithmetic, right_solve(): lax.linalg.triangular_solve(lower_factor, strip, left_side=False, lower=T...  39.4 us
    all_gather x2, blocking collectives, local(): whole_strip = lax.all_gather(panel_strip, 'col', axis=1, tiled=True)  37.6 us
  transfers between devices with their start and end apart: 7, of which 7 were waited for; matrix products, arithmetic and copies ran while one was open for 5% of the time, Pallas kernels for 0%

profile of v1, /device:TPU:1, one launch (start us, length us, event | category | flops | bytes accessed | tf_op | source)
XLA Modules:
  0.0 1241.3 jit_solution(6707079014376973267)
XLA Ops:
  7.2 19.7 %all_gather.47 = bf16[512,256]{0,1:T(8,128)(2,1)S(1)} all-gather(bf16[512,16]{0,1:T(8,128)(2,1)} %param.21), channel_id=1, replica_groups=mesh['row'=32,'col'=16] {'col'}, dimensions={1}, use_global_device_ids=true | all-gather | bytes 278528 | tf_op jit(solution)/shard_map/all_gather | solution.py:71
  26.9 15.4 %collective-permute-start = (bf16[512,256]{0,1:T(8,128)(2,1)S(1)}, bf16[512,256]{0,1:T(8,128)(2,1)S(1)}, u32[]{:S(2)}, u32[]{:S(2)}) collective-permute-start(bf16[512,256]{0,1:T(8,128)(2,1)S(1)} %all_gather.47), channel_id=1, source_target_pairs={{0,256},{16,272},{32,288},{48,304},{64,320},{80,336},{96,352},{112... | collective-permute-start | bytes 786440 | tf_op jit(solution)/shard_map/ppermute | solution.py:20
  42.3 0.8 fusion.46
  44.0 2.3 collective-permute-done
  47.3 1.2 broadcast_select_fusion.1
  48.5 0.7 all-gather.13.cloned.1.call-update
  50.1 0.7 compare_convert_fusion
  50.9 1.9 copy.30
  52.8 1.5 broadcast_multiply_fusion
  54.3 0.9 reshape.350
  55.2 118.6 %all-gather.11.cloned.1.call-done = bf16[32,512,512]{2,1,0:T(8,128)(2,1)} async-done(((bf16[1,512,512]{2,1,0:T(8,128)(2,1)}), bf16[32,512,512]{2,1,0:T(8,128)(2,1)}) %all-gather.11.cloned.1.call-update) | async-done | bytes 16777232 | tf_op jit(solution)/shard_map/all_gather | solution.py:13
  173.8 9.6 reduce_sum.72
  183.4 1.7 convolution_add_fusion.1
  185.1 95.5 %all-gather.13.cloned.1.call-done = bf16[32,512,512]{2,1,0:T(8,128)(2,1)} async-done(((bf16[1,512,512]{2,1,0:T(8,128)(2,1)}), bf16[32,512,512]{2,1,0:T(8,128)(2,1)}) %all-gather.13.cloned.1.call-update) | async-done | bytes 16777232 | tf_op jit(solution)/shard_map/all_gather | solution.py:13
  280.6 9.6 reduce_sum.73
  290.2 1.7 convolution_add_fusion
  291.9 0.9 copy-done.3
  292.9 18.8 %all_gather.51 = f32[512,256]{0,1:T(8,128)S(1)} all-gather(f32[512,16]{0,1:T(8,128)S(1)} %pad_maximum_fusion.1), channel_id=1, replica_groups=mesh['row'=32,'col'=16] {'col'}, dimensions={1}, use_global_device_ids=true | all-gather | bytes 557056 | tf_op jit(solution)/shard_map/all_gather | solution.py:122
  311.7 199.9 %all_gather.50 = f32[4096,16]{1,0:T(8,128)S(1)} all-gather(f32[8,16]{1,0:T(8,128)S(1)} %copy.33), channel_id=1, replica_groups=mesh['row'=32,'col'=16] {'row','col'}, dimensions={0}, use_global_device_ids=true | all-gather | bytes 262656 | tf_op jit(solution)/shard_map/all_gather | solution.py:115
  512.0 0.9 reshape.352
  513.1 11.7 cholesky.130
  525.5 9.8 custom-call.13
  535.8 12.1 cholesky.147
  550.1 4.0 while.10
  550.7 1.4 bitcast_dynamic-update-slice_fusion.4
  552.7 1.4 bitcast_dynamic-update-slice_fusion.4
  554.0 19.7 %custom-call.14 = f32[2,128,128]{1,2,0:T(8,128)S(1)} custom-call(f32[2,128,128]{2,1,0:T(8,128)S(1)} %get-tuple-element.90), custom_call_target="InvertDiagBlocksLowerTriangular" | custom-call | tf_op jit(solution)/shard_map/triangular_solve/custom-call.0 | solution.py:50
  575.5 0.8 broadcast_select_fusion.3
  577.0 1.7 pad_maximum_fusion
  578.7 73.2 %all-gather.17.cloned.1.call-done = bf16[16384,256]{0,1:T(8,128)(2,1)} async-done(((bf16[512,256]{0,1:T(8,128)(2,1)}), bf16[16384,256]{0,1:T(8,128)(2,1)}) %all-gather.17.cloned.1.call-update) | async-done | bytes 8388624 | tf_op jit(solution)/shard_map/all_gather | solution.py:13
  651.9 10.4 copy.52
  662.3 7.0 bitcast_reduce_fusion.2
  669.3 60.7 %all-gather.15.cloned.1.call-done = bf16[16384,256]{0,1:T(8,128)(2,1)} async-done(((bf16[512,256]{0,1:T(8,128)(2,1)}), bf16[16384,256]{0,1:T(8,128)(2,1)}) %all-gather.15.cloned.1.call-update) | async-done | bytes 8388624 | tf_op jit(solution)/shard_map/all_gather | solution.py:13
  730.1 10.4 copy.51
  740.5 7.3 bitcast_reduce_fusion.3
  747.8 1.6 convolution_subtract_fusion.1
  749.4 5.4 scatter.21
  754.8 1.6 convolution_subtract_fusion
  756.4 5.6 scatter.24
  762.2 18.8 %all_gather.57 = f32[512,256]{0,1:T(8,128)S(1)} all-gather(f32[512,16]{0,1:T(8,128)S(1)} %pad_maximum_fusion.2), channel_id=1, replica_groups=mesh['row'=32,'col'=16] {'col'}, dimensions={1}, use_global_device_ids=true | all-gather | bytes 557056 | tf_op jit(solution)/shard_map/all_gather | solution.py:122
  781.0 199.7 %all_gather.56 = f32[4096,16]{1,0:T(8,128)S(1)} all-gather(f32[8,16]{1,0:T(8,128)S(1)} %copy.38), channel_id=1, replica_groups=mesh['row'=32,'col'=16] {'row','col'}, dimensions={0}, use_global_device_ids=true | all-gather | bytes 262656 | tf_op jit(solution)/shard_map/all_gather | solution.py:115
  980.7 1.7 copy.39
  982.4 2.8 reshape.354
  986.2 11.7 cholesky.164
  998.5 9.8 custom-call.15
  1008.4 1.0 constant_dynamic-update-slice_fusion
  1009.4 1.1 convolution_subtract_fusion.6
  1010.5 11.7 cholesky.181
  1024.2 3.8 while.11
  1024.8 1.3 bitcast_dynamic-update-slice_fusion.5
  1026.8 1.3 bitcast_dynamic-update-slice_fusion.5
  1028.1 19.7 %custom-call.16 = f32[2,128,128]{1,2,0:T(8,128)S(1)} custom-call(f32[2,128,128]{2,1,0:T(8,128)S(1)} %get-tuple-element.91), custom_call_target="InvertDiagBlocksLowerTriangular" | custom-call | tf_op jit(solution)/shard_map/triangular_solve/custom-call.0 | solution.py:50
  1049.8 0.9 broadcast_select_fusion.2
  1051.9 73.0 %all-gather.21.cloned.1.call-done = bf16[16384,256]{0,1:T(8,128)(2,1)} async-done(((bf16[512,256]{0,1:T(8,128)(2,1)}), bf16[16384,256]{0,1:T(8,128)(2,1)}) %all-gather.21.cloned.1.call-update) | async-done | bytes 8388624 | tf_op jit(solution)/shard_map/all_gather | solution.py:13
  1124.9 10.4 copy.54
  1135.3 7.7 bitcast_reduce_fusion
  1143.0 60.0 %all-gather.19.cloned.1.call-done = bf16[16384,256]{0,1:T(8,128)(2,1)} async-done(((bf16[512,256]{0,1:T(8,128)(2,1)}), bf16[16384,256]{0,1:T(8,128)(2,1)}) %all-gather.19.cloned.1.call-update) | async-done | bytes 8388624 | tf_op jit(solution)/shard_map/all_gather | solution.py:13
  1203.1 10.4 copy.53
  1213.5 7.2 bitcast_reduce_fusion.1
  1221.4 3.3 scatter.26
  1224.7 1.6 convolution_subtract_fusion.2
  1226.3 3.5 scatter.29
  1229.8 1.6 and_select_fusion
  1231.4 2.9 copy.45
  (97 shorter events, 16.3 us)
Async XLA Ops:
  7.2 166.6 %all-gather.11.cloned.1.call-start = ((), (), s32[]{:S(2)}) async-start(), calls=%async_computation | async-start | bytes 17301504 | tf_op jit(solution)/shard_map/all_gather | solution.py:13
  26.9 19.5 %collective-permute-start = (bf16[512,256]{0,1:T(8,128)(2,1)S(1)}, bf16[512,256]{0,1:T(8,128)(2,1)S(1)}, u32[]{:S(2)}, u32[]{:S(2)}) collective-permute-start(bf16[512,256]{0,1:T(8,128)(2,1)S(1)} %all_gather.47), channel_id=1, source_target_pairs={{0,256},{16,272},{32,288},{48,304},{64,320},{80,336},{96,352},{112... | collective-permute-start | bytes 786440 | tf_op jit(solution)/shard_map/ppermute | solution.py:20
  46.7 2.8 copy-start.5
  48.5 232.1 %all-gather.13.cloned.1.call-start = ((), (), s32[]{:S(2)}) async-start(), calls=%async_computation.1 | async-start | bytes 17301504 | tf_op jit(solution)/shard_map/all_gather | solution.py:13
  49.2 602.7 %all-gather.17.cloned.1.call-start = ((), (), s32[]{:S(2)}) async-start(), calls=%async_computation.3 | async-start | bytes 8650752 | tf_op jit(solution)/shard_map/all_gather | solution.py:13
  55.2 128.2 %copy-start.2 = (f32[512,1024]{0,1:T(8,128)S(1)}, f32[512,1024]{0,1:T(8,128)}, u32[]{:S(2)}) copy-start(f32[512,1024]{0,1:T(8,128)} %broadcast_multiply_fusion) | copy-start | bytes 6291460
  185.1 106.8 %copy-start = (f32[512,512]{0,1:T(8,128)}, f32[512,512]{0,1:T(8,128)S(1)}, u32[]{:S(2)}) copy-start(f32[512,512]{0,1:T(8,128)S(1)} %convolution_add_fusion.1) | copy-start | bytes 3145732
  291.8 1.0 copy-start.3
  576.3 153.8 %all-gather.15.cloned.1.call-start = ((), (), s32[]{:S(2)}) async-start(), calls=%async_computation.2 | async-start | bytes 8650752 | tf_op jit(solution)/shard_map/all_gather | solution.py:13
  576.9 548.0 %all-gather.21.cloned.1.call-start = ((), (), s32[]{:S(2)}) async-start(), calls=%async_computation.5 | async-start | bytes 8650752 | tf_op jit(solution)/shard_map/all_gather | solution.py:13
  740.5 7.3 copy-start.1
  985.4 0.7 copy-start.4
  1050.6 152.4 %all-gather.19.cloned.1.call-start = ((), (), s32[]{:S(2)}) async-start(), calls=%async_computation.4 | async-start | bytes 8650752 | tf_op jit(solution)/shard_map/all_gather | solution.py:13
Sparse Core Ops, SparseCore 0:
  48.6 125.1 all-gather.10
  175.9 104.6 all-gather.12
  576.4 75.4 all-gather.16
  653.9 76.1 all-gather.14
  1050.8 74.0 all-gather.20
  1126.9 76.1 all-gather.18
